TPU v7x, 32 devices: a whole 2x2x4 slice. The times are simulated.
32 devices in a mesh: shard: 2 (over y), ctx: 4 (over x, core), tp: 4 (over z).
Axes of the slice: x: 2, y: 2, z: 4, core: 2. Of those that a mesh axis runs over, the one named last changes fastest.
Arguments:
- tokens: bfloat16 [2, 2, 2560, 1280], P(None, 'shard', ('ctx', 'tp')), may hold values from -0.16992188 to 0.16992188
- parents: int32 [2, 2, 40], P(None, 'shard'), may hold values from 0 to 38, as said below
- slot_segment: int32 [2, 2, 40], P(None, 'shard'), may hold values from 0 to 39, each once within a row
- w_query: bfloat16 [1280, 1280], P(('shard', 'ctx'), 'tp'), may hold values from -0.15625 to 0.15625
- w_key: bfloat16 [1280, 1280], P(('shard', 'ctx'), 'tp'), may hold values from -0.15625 to 0.15625
- w_value: bfloat16 [1280, 1280], P(('shard', 'ctx'), 'tp'), may hold values from -0.15625 to 0.15625
- w_attn_out: bfloat16 [1280, 1280], P('tp', ('shard', 'ctx')), may hold values from -0.15625 to 0.15625
- w_up: bfloat16 [1280, 5120], P(('shard', 'ctx'), 'tp'), may hold values from -0.15625 to 0.15625
- w_gate: bfloat16 [1280, 5120], P(('shard', 'ctx'), 'tp'), may hold values from -0.15625 to 0.15625
- w_down: bfloat16 [5120, 1280], P('tp', ('shard', 'ctx')), may hold values from -0.078125 to 0.078125
- alpha_attn: float32 [1280], replicated, may hold values from 0.15 to 0.6
- alpha_mlp: float32 [1280], replicated, may hold values from 0.15 to 0.6
- scale_qk: float32 [1280], P('tp'), may hold values from 0.7 to 1.4
- scale_up: float32 [5120], P('tp'), may hold values from 0.5 to 2
- scale_gate: float32 [5120], P('tp'), may hold values from 0.5 to 2
- cotangent: bfloat16 [2, 2, 2560, 1280], P(None, 'shard', ('ctx', 'tp')), may hold values from -6 to 6
Outputs:
- block_out: bfloat16 [2, 2, 2560, 1280], P(None, 'shard', ('ctx', 'tp'))
- grad_tokens: float32 [2, 2, 2560, 1280], P(None, 'shard', ('ctx', 'tp'))
- grad_w_query: float32 [1280, 1280], P(('shard', 'ctx'), 'tp')
- grad_w_key: float32 [1280, 1280], P(('shard', 'ctx'), 'tp')
- grad_w_value: float32 [1280, 1280], P(('shard', 'ctx'), 'tp')
- grad_w_attn_out: float32 [1280, 1280], P('tp', ('shard', 'ctx'))
- grad_w_up: float32 [1280, 5120], P(('shard', 'ctx'), 'tp')
- grad_w_gate: float32 [1280, 5120], P(('shard', 'ctx'), 'tp')
- grad_w_down: float32 [5120, 1280], P('tp', ('shard', 'ctx'))
- grad_alpha_attn: float32 [1280], replicated
- grad_alpha_mlp: float32 [1280], replicated
- grad_scale_qk: float32 [1280], P('tp')
- grad_scale_up: float32 [5120], P('tp')
- grad_scale_gate: float32 [5120], P('tp')
Inputs may be any that keep to these rules, and one draw needn't show every extreme that they name: `parents`: segment 0 of each tree is its root and names itself; every other segment names a segment with a lower number; every segment has 64 tokens. `slot_segment`: each tree's 40 slots hold its segments, each once.
All inputs are finite; a program needn't handle non-finite values.
Results may differ from a plain program's by a relative error of at most 0.019.
Values may be sent and summed in bfloat16 or wider, within the bound.
No kernel may reach another device: no remote copies, remote signals or barrier semaphores. Data moves between devices by JAX's collectives and lax.ppermute only.
A program may use at most 120 MiB of HBM per device.

v0:
```python
import math
import jax
import jax.numpy as jnp
from jax import lax
from jax.sharding import PartitionSpec as P

D = 1280
HDIM = 64
SEG = 64
SEGS = 40
TREE_TOK = 2560
EPSILON = 1e-06
MASKED = -1e30
HIGHEST = lax.Precision.HIGHEST


def unit_rows(values):
    return values * lax.rsqrt(jnp.sum(values * values, axis=-1, keepdims=True) + EPSILON)


def unit_heads(values):
    shaped = values.reshape(values.shape[0], values.shape[1] // HDIM, HDIM)
    return unit_rows(shaped).reshape(values.shape)


def contract_rows(former, latter):
    return lax.dot_general(
        former, latter, (((0,), (0,)), ((), ())), preferred_element_type=jnp.float32
    )


def contract_cols(former, latter):
    return lax.dot_general(
        former, latter, (((1,), (1,)), ((), ())), preferred_element_type=jnp.float32
    )


def split_heads(values):
    return values.reshape(values.shape[0], values.shape[1] // HDIM, HDIM).transpose(1, 0, 2)


def merge_heads(values):
    return values.transpose(1, 0, 2).reshape(values.shape[1], values.shape[0] * values.shape[2])


def mix_rows(residual, branch, mixing):
    return unit_rows(residual + mixing * (unit_rows(branch) - residual))


def query_key(query_raw, key_raw, gain_qk):
    return (unit_heads(query_raw) * gain_qk, unit_heads(key_raw) * gain_qk)


def middle(up_raw, gate_raw, scale_up, scale_gate):
    return up_raw * scale_up * jax.nn.silu(gate_raw * (scale_gate * math.sqrt(D)))


def group_rows(own_block):
    return lax.all_gather(own_block, "tp", axis=0, tiled=True)


def group_grads(own_block):
    return lax.all_gather(own_block, "tp", axis=0, tiled=True)


def own_rows(partial_value):
    return own_grads(partial_value)


def own_grads(partial_value):
    return lax.psum_scatter(
        partial_value.astype(jnp.bfloat16), "tp", scatter_dimension=0, tiled=True
    ).astype(jnp.float32)


def visibility(parents, slots, group_size):
    labels = jnp.arange(SEGS, dtype=jnp.int32)
    linked = (parents[:, None] == labels[None, :]).astype(jnp.float32)
    reachable = jnp.maximum(linked, jnp.eye(SEGS, dtype=jnp.float32))
    for doubling in range(SEGS.bit_length()):
        reachable = jnp.minimum(jnp.dot(reachable, reachable, precision=HIGHEST), 1.0)
    segment = jnp.broadcast_to(slots[:, None], (SEGS, SEG)).reshape(TREE_TOK)
    offset = lax.broadcasted_iota(jnp.int32, (SEGS, SEG), 1).reshape(TREE_TOK)
    first_row = lax.axis_index("ctx") * group_size
    seg_query = lax.dynamic_slice_in_dim(segment, first_row, group_size)
    off_query = lax.dynamic_slice_in_dim(offset, first_row, group_size)
    key_onehot = (segment[:, None] == labels[None, :]).astype(jnp.float32)
    query_onehot = (seg_query[:, None] == labels[None, :]).astype(jnp.float32)
    linked_rows = jnp.dot(query_onehot, reachable, precision=HIGHEST)
    seen = (
        lax.dot_general(linked_rows, key_onehot, (((1,), (1,)), ((), ())), precision=HIGHEST) > 0.5
    )
    return seen & (
        (seg_query[:, None] != segment[None, :]) | (offset[None, :] <= off_query[:, None])
    )


def forward_attention(gathered, vectors, tokens_own, parents, slots):
    w_query, w_key, w_value, w_attn_out = gathered[:4]
    alpha_attn, alpha_mlp, scale_qk, scale_up, scale_gate = vectors
    score_scale = math.sqrt(HDIM)
    hidden_group = group_rows(tokens_own)
    visible = visibility(parents, slots, hidden_group.shape[0])
    query_raw = jnp.dot(hidden_group, w_query, preferred_element_type=jnp.float32)
    key_raw = jnp.dot(hidden_group, w_key, preferred_element_type=jnp.float32)
    value_low = jnp.dot(hidden_group, w_value, preferred_element_type=jnp.float32).astype(
        jnp.bfloat16
    )
    query_unit, key_unit = query_key(query_raw, key_raw, scale_qk)
    queries = query_unit.astype(jnp.bfloat16)
    keys_own = key_unit.astype(jnp.bfloat16)
    keys_values = lax.all_gather(
        jnp.concatenate([keys_own, value_low], axis=1), "ctx", axis=0, tiled=True
    )
    keys_tree, values_tree = jnp.split(keys_values, 2, axis=1)
    query_heads = split_heads(queries)
    key_heads = split_heads(keys_tree)
    value_heads = split_heads(values_tree)

    def head_forward(record):
        query_one, key_one, value_one = record
        scores = jnp.where(visible, contract_cols(query_one, key_one) * score_scale, MASKED)
        row_peak = jnp.max(scores, axis=-1, keepdims=True)
        lifted = jnp.exp(scores - row_peak)
        row_total = jnp.sum(lifted, axis=-1, keepdims=True)
        soft_weights = lifted / row_total
        head_value = jnp.dot(
            soft_weights.astype(jnp.bfloat16), value_one, preferred_element_type=jnp.float32
        )
        return (head_value, (row_peak + jnp.log(row_total))[:, 0])

    head_values, log_totals = lax.map(head_forward, (query_heads, key_heads, value_heads))
    heads_low = merge_heads(head_values).astype(jnp.bfloat16)
    branch_one = own_rows(jnp.dot(heads_low, w_attn_out, preferred_element_type=jnp.float32))
    kept = (
        hidden_group,
        visible,
        query_raw,
        key_raw,
        query_heads,
        key_heads,
        value_heads,
        log_totals,
        heads_low,
    )
    return (branch_one, kept)


def feed_forward(gathered, vectors, tokens_own, branch_one, cotangent_own):
    w_up, w_gate, w_down = gathered[4:]
    alpha_attn, alpha_mlp, scale_qk, scale_up, scale_gate = vectors
    tokens_wide = tokens_own.astype(jnp.float32)
    hidden_one = mix_rows(tokens_wide, branch_one, alpha_attn)
    hidden_one_group = group_rows(hidden_one.astype(jnp.bfloat16))
    up_raw = jnp.dot(hidden_one_group, w_up, preferred_element_type=jnp.float32)
    gate_raw = jnp.dot(hidden_one_group, w_gate, preferred_element_type=jnp.float32)
    mixed_low = middle(up_raw, gate_raw, scale_up, scale_gate).astype(jnp.bfloat16)
    branch_two = own_rows(jnp.dot(mixed_low, w_down, preferred_element_type=jnp.float32))
    output_wide, pull_out = jax.vjp(mix_rows, hidden_one, branch_two, alpha_mlp)
    upstream = cotangent_own.astype(jnp.float32)
    hidden_one_direct, branch_two_grad, grad_alpha_mlp = pull_out(upstream)
    branch_two_group = group_grads(branch_two_grad.astype(jnp.bfloat16))
    mixed_grad = contract_cols(branch_two_group, w_down).astype(jnp.bfloat16).astype(jnp.float32)
    middle_value, pull_mid = jax.vjp(middle, up_raw, gate_raw, scale_up, scale_gate)
    up_grad, gate_grad, grad_scale_up, grad_scale_gate = pull_mid(mixed_grad)
    up_low = up_grad.astype(jnp.bfloat16)
    gate_low = gate_grad.astype(jnp.bfloat16)
    hidden_one_grad = hidden_one_direct + own_grads(
        contract_cols(up_low, w_up) + contract_cols(gate_low, w_gate)
    )
    hidden_again, pull_in = jax.vjp(mix_rows, tokens_wide, branch_one, alpha_attn)
    tokens_direct, branch_one_grad, grad_alpha_attn = pull_in(hidden_one_grad)
    factors = (mixed_low, branch_two_group, hidden_one_group, up_low, gate_low)
    sums = (grad_alpha_attn, grad_alpha_mlp, grad_scale_up, grad_scale_gate)
    return (output_wide.astype(jnp.bfloat16), tokens_direct, branch_one_grad, factors, sums)


def backward_attention(gathered, vectors, kept, branch_one_grad, tokens_direct):
    w_query, w_key, w_value, w_attn_out = gathered[:4]
    scale_qk = vectors[2]
    score_scale = math.sqrt(HDIM)
    (
        hidden_group,
        visible,
        query_raw,
        key_raw,
        query_heads,
        key_heads,
        value_heads,
        log_totals,
        heads_low,
    ) = kept
    branch_one_group = group_grads(branch_one_grad.astype(jnp.bfloat16))
    heads_grad = split_heads(contract_cols(branch_one_group, w_attn_out).astype(jnp.bfloat16))

    def head_backward(record):
        query_one, key_one, value_one, upstream_one, log_total = record
        scores = jnp.where(visible, contract_cols(query_one, key_one) * score_scale, MASKED)
        soft_weights = jnp.exp(scores - log_total[:, None])
        weight_grad = contract_cols(upstream_one, value_one)
        row_inner = jnp.sum(soft_weights * weight_grad, axis=-1, keepdims=True)
        score_grad = (soft_weights * (weight_grad - row_inner)).astype(jnp.bfloat16)
        query_grad = jnp.dot(score_grad, key_one, preferred_element_type=jnp.float32) * score_scale
        key_grad = contract_rows(score_grad, query_one) * score_scale
        value_grad = contract_rows(soft_weights.astype(jnp.bfloat16), upstream_one)
        return (query_grad, key_grad, value_grad)

    query_grads, key_grads, value_grads = lax.map(
        head_backward, (query_heads, key_heads, value_heads, heads_grad, log_totals)
    )
    both = lax.psum_scatter(
        jnp.concatenate([merge_heads(key_grads), merge_heads(value_grads)], axis=1).astype(
            jnp.bfloat16
        ),
        "ctx",
        scatter_dimension=0,
        tiled=True,
    ).astype(jnp.float32)
    key_own_grad, value_own_grad = jnp.split(both, 2, axis=1)
    unit_again, pull_qk = jax.vjp(query_key, query_raw, key_raw, scale_qk)
    query_raw_grad, key_raw_grad, grad_scale_qk = pull_qk((merge_heads(query_grads), key_own_grad))
    query_low = query_raw_grad.astype(jnp.bfloat16)
    key_low = key_raw_grad.astype(jnp.bfloat16)
    value_grad_low = value_own_grad.astype(jnp.bfloat16)
    input_part = (
        contract_cols(query_low, w_query)
        + contract_cols(key_low, w_key)
        + contract_cols(value_grad_low, w_value)
    )
    grad_tokens = tokens_direct + own_grads(input_part)
    factors = (hidden_group, query_low, key_low, value_grad_low, heads_low, branch_one_group)
    return (grad_tokens, factors, grad_scale_qk)


def per_device(
    tokens,
    parents,
    slot_segment,
    w_query,
    w_key,
    w_value,
    w_attn_out,
    w_up,
    w_gate,
    w_down,
    alpha_attn,
    alpha_mlp,
    scale_qk,
    scale_up,
    scale_gate,
    cotangent,
):
    local_heads = w_query.shape[1]
    local_hidden = w_up.shape[1]
    vectors = (alpha_attn, alpha_mlp, scale_qk, scale_up, scale_gate)
    spread = ("shard", "ctx")
    gathered = (
        lax.all_gather(w_query, spread, axis=0, tiled=True),
        lax.all_gather(w_key, spread, axis=0, tiled=True),
        lax.all_gather(w_value, spread, axis=0, tiled=True),
        lax.all_gather(w_attn_out, spread, axis=1, tiled=True),
        lax.all_gather(w_up, spread, axis=0, tiled=True),
        lax.all_gather(w_gate, spread, axis=0, tiled=True),
        lax.all_gather(w_down, spread, axis=1, tiled=True),
    )
    micros = range(tokens.shape[0])
    front = [
        forward_attention(gathered, vectors, tokens[m, 0], parents[m, 0], slot_segment[m, 0])
        for m in micros
    ]
    mid = [
        feed_forward(gathered, vectors, tokens[m, 0], front[m][0], cotangent[m, 0]) for m in micros
    ]
    back = [
        backward_attention(gathered, vectors, front[m][1], mid[m][2], mid[m][1]) for m in micros
    ]

    def stack(pick):
        return jnp.concatenate([pick(m) for m in micros], axis=0)

    mixed_all, top_all, hidden_all, up_all, gate_all = (
        stack(lambda m: mid[m][3][place]) for place in range(5)
    )
    tokens_all, query_all, key_all, value_all, heads_all, branch_all = (
        stack(lambda m: back[m][1][place]) for place in range(6)
    )

    def to_owner(former, latter, axis):
        product = contract_rows(former, latter).astype(jnp.bfloat16)
        return lax.psum_scatter(product, spread, scatter_dimension=axis, tiled=True).astype(
            jnp.float32
        )

    grad_d = to_owner(mixed_all, top_all, 1)
    grad_u = to_owner(hidden_all, up_all, 0)
    grad_g = to_owner(hidden_all, gate_all, 0)
    grad_o = to_owner(heads_all, branch_all, 1)
    grad_q = to_owner(tokens_all, query_all, 0)
    grad_k = to_owner(tokens_all, key_all, 0)
    grad_v = to_owner(tokens_all, value_all, 0)
    sum_attn, sum_mlp, sum_up, sum_gate = (
        sum((mid[m][4][place] for m in micros)) for place in range(4)
    )
    sum_qk = sum((back[m][2] for m in micros))
    tp_count = lax.axis_size("tp")
    tp_place = lax.axis_index("tp")

    def padded(vector):
        return lax.dynamic_update_slice_in_dim(
            jnp.zeros((vector.shape[0] * tp_count,), jnp.float32),
            vector,
            tp_place * vector.shape[0],
            0,
        )

    alpha_attn_sum, alpha_mlp_sum, qk_sum, up_sum, gate_sum = lax.psum(
        (sum_attn, sum_mlp, padded(sum_qk), padded(sum_up), padded(sum_gate)),
        ("shard", "ctx", "tp"),
    )
    return (
        jnp.stack([mid[m][0] for m in micros])[:, None],
        jnp.stack([back[m][0] for m in micros])[:, None],
        grad_q,
        grad_k,
        grad_v,
        grad_o,
        grad_u,
        grad_g,
        grad_d,
        alpha_attn_sum,
        alpha_mlp_sum,
        lax.dynamic_slice_in_dim(qk_sum, tp_place * local_heads, local_heads),
        lax.dynamic_slice_in_dim(up_sum, tp_place * local_hidden, local_hidden),
        lax.dynamic_slice_in_dim(gate_sum, tp_place * local_hidden, local_hidden),
    )


def solution(mesh):
    return jax.shard_map(
        per_device,
        mesh=mesh,
        in_specs=(
            P(None, "shard", ("ctx", "tp"), None),
            P(None, "shard", None),
            P(None, "shard", None),
            P(("shard", "ctx"), "tp"),
            P(("shard", "ctx"), "tp"),
            P(("shard", "ctx"), "tp"),
            P("tp", ("shard", "ctx")),
            P(("shard", "ctx"), "tp"),
            P(("shard", "ctx"), "tp"),
            P("tp", ("shard", "ctx")),
            P(),
            P(),
            P("tp"),
            P("tp"),
            P("tp"),
            P(None, "shard", ("ctx", "tp"), None),
        ),
        out_specs=(
            P(None, "shard", ("ctx", "tp"), None),
            P(None, "shard", ("ctx", "tp"), None),
            P(("shard", "ctx"), "tp"),
            P(("shard", "ctx"), "tp"),
            P(("shard", "ctx"), "tp"),
            P("tp", ("shard", "ctx")),
            P(("shard", "ctx"), "tp"),
            P(("shard", "ctx"), "tp"),
            P("tp", ("shard", "ctx")),
            P(),
            P(),
            P("tp"),
            P("tp"),
            P("tp"),
        ),
        check_vma=False,
    )
```

profile of v0, /device:TPU:0, one launch (start us, length us, event | category | flops | bytes accessed | tf_op | source)
XLA Modules:
  0.0 1370.7 jit_solution(1674269570403214196)
XLA Ops:
  54.6 36.5 %all-gather.38.cloned.1.call-done = bf16[1,1,640,1280]{3,2,1,0:T(8,128)(2,1)} async-done(((bf16[1,1,160,1280]{3,2,1,0:T(8,128)(2,1)}), bf16[1,1,640,1280]{3,2,1,0:T(8,128)(2,1)}) %all-gather.38.cloned.1.call-update) | async-done | bytes 1638416 | tf_op jit(solution)/shard_map/all_gather | solution.py:59
  150.4 57.9 %while.52 = (s32[]{:T(128)}, bf16[5,640,64]{1,2,0:T(8,128)(2,1)}, f32[5,640]{1,0:T(8,128)}, bf16[5,640,64]{2,1,0:T(8,128)(2,1)}, bf16[5,2560,64]{2,1,0:T(8,128)(...) while((s32[]{:T(128)}, bf16[5,640,64]{1,2,0:T(8,128)(2,1)}, ...), condition=%wide.region_5.6_spmd, body=%wide.region_2.5_spmd.sunk | while | flops 432536960 | bytes 49184892 | solution.py:132
  213.1 33.7 %reduce-scatter.22.cloned.1.call-done = bf16[160,1280]{1,0:T(8,128)(2,1)} async-done(((bf16[640,1280]{1,0:T(8,128)(2,1)}), bf16[160,1280]{1,0:T(8,128)(2,1)}) %reduce-scatter.22.cloned.1.call-update) | async-done | bytes 409616 | tf_op jit(solution)/shard_map/reduce_scatter | solution.py:71
  257.4 32.3 %all-gather.18.cloned.1.call-done = bf16[640,1280]{1,0:T(8,128)(2,1)} async-done(((bf16[160,1280]{1,0:T(8,128)(2,1)}), bf16[640,1280]{1,0:T(8,128)(2,1)}) %all-gather.18.cloned.1.call-update) | async-done | bytes 1638416 | tf_op jit(solution)/shard_map/all_gather | solution.py:59
  296.3 27.0 %all-gather.20.cloned.1.call-done = bf16[1280,1280]{1,0:T(8,128)(2,1)} async-done(((bf16[160,1280]{1,0:T(8,128)(2,1)}), bf16[1280,1280]{1,0:T(8,128)(2,1)}) %all-gather.20.cloned.1.call-update) | async-done | bytes 3276816 | tf_op jit(solution)/shard_map/all_gather | solution.py:262
  330.9 27.2 %all-gather.24.cloned.1.call-done = bf16[1280,1280]{0,1:T(8,128)(2,1)} async-done(((bf16[1280,160]{0,1:T(8,128)(2,1)}), bf16[1280,1280]{0,1:T(8,128)(2,1)}) %all-gather.24.cloned.1.call-update) | async-done | bytes 3276816 | tf_op jit(solution)/shard_map/all_gather | solution.py:264
  371.1 17.7 %all-gather.26.cloned.1.call-done = bf16[2560,640]{0,1:T(8,128)(2,1)} async-done(((bf16[640,640]{0,1:T(8,128)(2,1)}), bf16[2560,640]{0,1:T(8,128)(2,1)}) %all-gather.26.cloned.1.call-update) | async-done | bytes 3276816 | tf_op jit(solution)/shard_map/all_gather | solution.py:112
  409.0 51.8 %while.53 = (s32[]{:T(128)}, bf16[5,640,64]{1,2,0:T(8,128)(2,1)}, f32[5,640]{1,0:T(8,128)S(1)}, bf16[5,640,64]{2,1,0:T(8,128)(2,1)}, bf16[5,2560,64]{2,1,0:T(8,1...) while((s32[]{:T(128)}, bf16[5,640,64]{1,2,0:T(8,128)(2,1)}, ...), condition=%wide.region_17.18_spmd, body=%wide.region_14.17_spmd.sunk | while | flops 432536960 | bytes 49184892 | solution.py:132
  502.6 36.5 %reduce-scatter.30.cloned.1.call-done = bf16[160,1280]{1,0:T(8,128)(2,1)} async-done(((bf16[640,1280]{1,0:T(8,128)(2,1)}), bf16[160,1280]{1,0:T(8,128)(2,1)}) %reduce-scatter.30.cloned.1.call-update) | async-done | bytes 409616 | tf_op jit(solution)/shard_map/reduce_scatter | solution.py:71
  543.0 37.1 %all-gather.28.cloned.1.call-done = bf16[640,1280]{1,0:T(8,128)(2,1)} async-done(((bf16[160,1280]{1,0:T(8,128)(2,1)}), bf16[640,1280]{1,0:T(8,128)(2,1)}) %all-gather.28.cloned.1.call-update) | async-done | bytes 1638416 | tf_op jit(solution)/shard_map/all_gather | solution.py:59
  594.0 35.3 %reduce-scatter.28.cloned.1.call-done = bf16[160,1280]{1,0:T(8,128)(2,1)} async-done(((bf16[640,1280]{1,0:T(8,128)(2,1)}), bf16[160,1280]{1,0:T(8,128)(2,1)}) %reduce-scatter.28.cloned.1.call-update) | async-done | bytes 409616 | tf_op jit(solution)/shard_map/reduce_scatter | solution.py:71
  636.0 36.7 %all-gather.34.cloned.1.call-done = bf16[640,1280]{1,0:T(8,128)(2,1)} async-done(((bf16[160,1280]{1,0:T(8,128)(2,1)}), bf16[640,1280]{1,0:T(8,128)(2,1)}) %all-gather.34.cloned.1.call-update) | async-done | bytes 1638416 | tf_op jit(solution)/shard_map/all_gather | solution.py:63
  690.5 35.2 %reduce-scatter.34.cloned.1.call-done = bf16[160,1280]{1,0:T(8,128)(2,1)} async-done(((bf16[640,1280]{1,0:T(8,128)(2,1)}), bf16[160,1280]{1,0:T(8,128)(2,1)}) %reduce-scatter.34.cloned.1.call-update) | async-done | bytes 409616 | tf_op jit(solution)/shard_map/reduce_scatter | solution.py:71
  734.0 34.7 %all-gather.32.cloned.1.call-done = bf16[640,1280]{1,0:T(8,128)(2,1)} async-done(((bf16[160,1280]{1,0:T(8,128)(2,1)}), bf16[640,1280]{1,0:T(8,128)(2,1)}) %all-gather.32.cloned.1.call-update) | async-done | bytes 1638416 | tf_op jit(solution)/shard_map/all_gather | solution.py:63
  775.3 71.4 %while.54 = (s32[]{:T(128)}, f32[5,640,64]{1,2,0:T(8,128)S(1)}, bf16[5,2560,64]{1,2,0:T(8,128)(2,1)}, bf16[5,2560,64]{1,2,0:T(8,128)(2,1)}, bf16[5,640,64]{2,1,0...) while((s32[]{:T(128)}, f32[5,640,64]{1,2,0:T(8,128)S(1)}, ...), condition=%wide.region_31.32_spmd, body=%wide.region_29.31_spmd.sunk | while | flops 1063525760 | bytes 61458068 | solution.py:208
  860.6 71.4 %while.55 = (s32[]{:T(128)}, f32[5,640,64]{1,2,0:T(8,128)S(1)}, bf16[5,2560,64]{1,2,0:T(8,128)(2,1)}, bf16[5,2560,64]{1,2,0:T(8,128)(2,1)}, bf16[5,640,64]{2,1,0...) while((s32[]{:T(128)}, f32[5,640,64]{1,2,0:T(8,128)S(1)}, ...), condition=%wide.region_43.44_spmd, body=%wide.region_41.43_spmd.sunk | while | flops 1063525760 | bytes 61458068 | solution.py:208
  1028.6 48.3 %reduce-scatter.48.cloned.1.call-done = bf16[160,1280]{1,0:T(8,128)(2,1)} async-done(((bf16[1280,1280]{1,0:T(8,128)(2,1)}), bf16[160,1280]{1,0:T(8,128)(2,1)}) %reduce-scatter.48.cloned.1.call-update) | async-done | bytes 409616 | tf_op jit(solution)/shard_map/reduce_scatter | solution.py:290
  1078.8 48.2 %reduce-scatter.46.cloned.1.call-done = bf16[160,1280]{1,0:T(8,128)(2,1)} async-done(((bf16[1280,1280]{1,0:T(8,128)(2,1)}), bf16[160,1280]{1,0:T(8,128)(2,1)}) %reduce-scatter.46.cloned.1.call-update) | async-done | bytes 409616 | tf_op jit(solution)/shard_map/reduce_scatter | solution.py:290
  1129.1 36.7 %reduce-scatter.44.cloned.1.call-done = bf16[320,160]{0,1:T(8,128)(2,1)} async-done(((bf16[320,1280]{0,1:T(8,128)(2,1)}), bf16[320,160]{0,1:T(8,128)(2,1)}) %reduce-scatter.44.cloned.1.call-update) | async-done | bytes 102416 | tf_op jit(solution)/shard_map/reduce_scatter | solution.py:290
  1167.5 37.6 %reduce-scatter.38.cloned.1.call-done = bf16[160,320]{1,0:T(8,128)(2,1)} async-done(((bf16[1280,320]{1,0:T(8,128)(2,1)}), bf16[160,320]{1,0:T(8,128)(2,1)}) %reduce-scatter.38.cloned.1.call-update) | async-done | bytes 102416 | tf_op jit(solution)/shard_map/reduce_scatter | solution.py:290
  1206.7 40.9 %all-reduce = (f32[1280]{0:T(1024)}, f32[1280]{0:T(1024)}, f32[1280]{0:T(1024)S(1)}, f32[5120]{0:T(1024)S(1)}, f32[5120]{0:T(1024)S(1)}) all-reduce(f32[1280]{0:T(1024)S(1)} %add.328, f32[1280]{0:T(1024)S(1)} %add.329, f32[1280]{0:T(1024)S(1)} %add_dynamic-update-slice_fusion.1, ...), channel_id=1, replica_groups=mesh['shard'=2,'ctx'=4,'tp'=4] {'shard','ctx','tp'}, use_global_device_ids=true, to_apply=%region_57.58 | all-reduce | flops 14080 | bytes 112640 | tf_op jit(solution)/shard_map/psum | solution.py:316
  1251.3 32.1 %reduce-scatter.40.cloned.1.call-done = bf16[160,320]{1,0:T(8,128)(2,1)} async-done(((bf16[1280,320]{1,0:T(8,128)(2,1)}), bf16[160,320]{1,0:T(8,128)(2,1)}) %reduce-scatter.40.cloned.1.call-update) | async-done | bytes 102416 | tf_op jit(solution)/shard_map/reduce_scatter | solution.py:290
  1285.0 36.9 %reduce-scatter.36.cloned.1.call-done = bf16[160,1280]{1,0:T(8,128)(2,1)} async-done(((bf16[640,1280]{1,0:T(8,128)(2,1)}), bf16[160,1280]{1,0:T(8,128)(2,1)}) %reduce-scatter.36.cloned.1.call-update) | async-done | bytes 409616 | tf_op jit(solution)/shard_map/reduce_scatter | solution.py:71
  1321.9 38.3 %reduce-scatter.32.cloned.1.call-done = bf16[160,1280]{1,0:T(8,128)(2,1)} async-done(((bf16[640,1280]{1,0:T(8,128)(2,1)}), bf16[160,1280]{1,0:T(8,128)(2,1)}) %reduce-scatter.32.cloned.1.call-update) | async-done | bytes 409616 | tf_op jit(solution)/shard_map/reduce_scatter | solution.py:71
  (656 shorter events, 643.6 us)
Async XLA Ops:
  10.2 80.9 %all-gather.38.cloned.1.call-start = ((), (), s32[]{:S(2)}) async-start(), calls=%async_computation.43 | async-start | bytes 2048000 | tf_op jit(solution)/shard_map/all_gather | solution.py:59
  11.0 128.2 %all-gather.16.cloned.1.call-start = ((), (), s32[]{:S(2)}) async-start(), calls=%async_computation.17 | async-start | bytes 4096000 | tf_op jit(solution)/shard_map/all_gather | solution.py:112
  108.4 138.4 %reduce-scatter.22.cloned.1.call-start = ((), (), s32[]{:S(2)}) async-start(), calls=%async_computation.18 | async-start | bytes 2048000 | tf_op jit(solution)/shard_map/reduce_scatter | solution.py:71
  253.2 104.8 %all-gather.24.cloned.1.call-start = ((), (), s32[]{:S(2)}) async-start(), calls=%async_computation.22 | async-start | bytes 3686400 | tf_op jit(solution)/shard_map/all_gather | solution.py:264
  254.0 134.9 %all-gather.26.cloned.1.call-start = ((), (), s32[]{:S(2)}) async-start(), calls=%async_computation.24 | async-start | bytes 4096000 | tf_op jit(solution)/shard_map/all_gather | solution.py:112
  257.3 144.4 %reduce-scatter.24.cloned.1.call-start = ((), (), s32[]{:S(2)}) async-start(), calls=%async_computation.23 | async-start | bytes 2048000 | tf_op jit(solution)/shard_map/reduce_scatter | solution.py:71
  364.0 101.3 %all-gather.30.cloned.1.call-start = ((), (), s32[]{:S(2)}) async-start(), calls=%async_computation.28 | async-start | bytes 2048000 | tf_op jit(solution)/shard_map/all_gather | solution.py:63
  409.0 92.4 %reduce-scatter.26.cloned.1.call-start = ((), (), s32[]{:S(2)}) async-start(), calls=%async_computation.25 | async-start | bytes 2048000 | tf_op jit(solution)/shard_map/reduce_scatter | solution.py:71
  483.8 96.4 %all-gather.28.cloned.1.call-start = ((), (), s32[]{:S(2)}) async-start(), calls=%async_computation.26 | async-start | bytes 2048000 | tf_op jit(solution)/shard_map/all_gather | solution.py:59
  543.0 86.3 %reduce-scatter.28.cloned.1.call-start = ((), (), s32[]{:S(2)}) async-start(), calls=%async_computation.27 | async-start | bytes 2048000 | tf_op jit(solution)/shard_map/reduce_scatter | solution.py:71
  594.0 78.7 %all-gather.34.cloned.1.call-start = ((), (), s32[]{:S(2)}) async-start(), calls=%async_computation.32 | async-start | bytes 2048000 | tf_op jit(solution)/shard_map/all_gather | solution.py:63
  635.5 90.2 %reduce-scatter.34.cloned.1.call-start = ((), (), s32[]{:S(2)}) async-start(), calls=%async_computation.33 | async-start | bytes 2048000 | tf_op jit(solution)/shard_map/reduce_scatter | solution.py:71
  731.5 121.9 %all-gather.36.cloned.1.call-start = ((), (), s32[]{:S(2)}) async-start(), calls=%async_computation.34 | async-start | bytes 2048000 | tf_op jit(solution)/shard_map/all_gather | solution.py:63
  733.7 245.9 %reduce-scatter.52.cloned.1.call-start = ((), (), s32[]{:S(2)}) async-start(), calls=%async_computation.45 | async-start | bytes 4096000
  853.2 128.9 %reduce-scatter.54.cloned.1.call-start = ((), (), s32[]{:S(2)}) async-start(), calls=%async_computation.46 | async-start | bytes 4096000
  938.5 88.2 %reduce-scatter.50.cloned.1.call-start = ((), (), s32[]{:S(2)}) async-start(), calls=%async_computation.42 | async-start | bytes 3686400 | tf_op jit(solution)/shard_map/reduce_scatter | solution.py:290
  948.3 128.6 %reduce-scatter.48.cloned.1.call-start = ((), (), s32[]{:S(2)}) async-start(), calls=%async_computation.41 | async-start | bytes 3686400 | tf_op jit(solution)/shard_map/reduce_scatter | solution.py:290
  959.0 168.0 %reduce-scatter.46.cloned.1.call-start = ((), (), s32[]{:S(2)}) async-start(), calls=%async_computation.40 | async-start | bytes 3686400 | tf_op jit(solution)/shard_map/reduce_scatter | solution.py:290
  968.8 197.0 %reduce-scatter.44.cloned.1.call-start = ((), (), s32[]{:S(2)}) async-start(), calls=%async_computation.39 | async-start | bytes 1105920 | tf_op jit(solution)/shard_map/reduce_scatter | solution.py:290
  974.1 230.9 %reduce-scatter.38.cloned.1.call-start = ((), (), s32[]{:S(2)}) async-start(), calls=%async_computation.36 | async-start | bytes 1105920 | tf_op jit(solution)/shard_map/reduce_scatter | solution.py:290
  979.1 270.6 %reduce-scatter.42.cloned.1.call-start = ((), (), s32[]{:S(2)}) async-start(), calls=%async_computation.38 | async-start | bytes 1105920 | tf_op jit(solution)/shard_map/reduce_scatter | solution.py:290
  990.3 293.1 %reduce-scatter.40.cloned.1.call-start = ((), (), s32[]{:S(2)}) async-start(), calls=%async_computation.37 | async-start | bytes 1105920 | tf_op jit(solution)/shard_map/reduce_scatter | solution.py:290
  1007.4 314.5 %reduce-scatter.36.cloned.1.call-start = ((), (), s32[]{:S(2)}) async-start(), calls=%async_computation.35 | async-start | bytes 2048000 | tf_op jit(solution)/shard_map/reduce_scatter | solution.py:71
  1012.5 347.7 %reduce-scatter.32.cloned.1.call-start = ((), (), s32[]{:S(2)}) async-start(), calls=%async_computation.31 | async-start | bytes 2048000 | tf_op jit(solution)/shard_map/reduce_scatter | solution.py:71
  (145 other events, 2729.2 us)
Sparse Core Ops, SparseCore 0:
  11.0 40.8 all-gather.39
  54.0 37.0 all-gather.37
  108.5 30.6 all-gather.15
  212.1 34.6 reduce-scatter.21
  364.1 36.2 reduce-scatter.23
  409.1 38.1 all-gather.29
  465.2 36.1 reduce-scatter.25
  503.8 35.3 reduce-scatter.29
  594.1 35.1 reduce-scatter.27
  690.6 35.1 reduce-scatter.33
  853.3 37.6 reduce-scatter.51
  938.6 37.6 reduce-scatter.53
  979.7 46.8 reduce-scatter.49
  1029.9 46.9 reduce-scatter.47
  1080.1 46.8 reduce-scatter.45
  1130.1 35.7 reduce-scatter.43
  1169.2 35.7 reduce-scatter.37
  1208.1 35.8 reduce-scatter.41
  1247.5 35.8 reduce-scatter.39
  1285.5 36.3 reduce-scatter.35
  1324.9 35.2 reduce-scatter.31
Sparse Core Ops, SparseCore 1:
  214.4 31.0 all-gather.21
  252.7 37.0 all-gather.17
  291.7 31.5 all-gather.19
  325.3 32.7 all-gather.23
  359.6 29.1 all-gather.25
  543.1 37.0 all-gather.27
  635.6 37.0 all-gather.33
  731.6 37.0 all-gather.31
  770.2 36.8 all-gather.35
where the time goes:
time: 1380 us; the launch traced here: 1370 us
  waiting for transfers between devices  707 us (51%)
  matrix products  354 us (26%)
  local copies, waits for them, and re-layouts  111 us (8%)
  blocking collectives  92.6 us (7%)
  other arithmetic  84.3 us (6%)
  between operations  17.7 us (1%)
    reduce_scatter x8, waiting for transfers between devices, own_grads(): lax.psum_scatter(partial_value.astype(jnp.bfloat16), 'tp', scatter_dimens...  234 us
    reduce_scatter x7, waiting for transfers between devices, to_owner(): lax.psum_scatter(product, spread, scatter_dimension=axis, tiled=True)  210 us
    dot_general x44, matrix products, contract_cols(): lax.dot_general(former, latter, (((1,), (1,)), ((), ())), preferred_eleme...  127 us
    all_gather x4, waiting for transfers between devices, group_rows(): return lax.all_gather(own_block, 'tp', axis=0, tiled=True)  110 us
    dot_general x27, matrix products, contract_rows(): lax.dot_general(former, latter, (((0,), (0,)), ((), ())), preferred_eleme...  88.9 us
    all_gather x4, waiting for transfers between devices, group_grads(): return lax.all_gather(own_block, 'tp', axis=0, tiled=True)  71.4 us
    dot_general x10, matrix products, head_forward(): jnp.dot(soft_weights.astype(jnp.bfloat16), value_one, preferred_element_t...  49.6 us
    psum x1, blocking collectives, per_device(): lax.psum((sum_attn, sum_mlp, padded(sum_qk), padded(sum_up), padded(sum_g...  40.9 us
  transfers between devices with their start and end apart: 30, of which 23 were waited for; matrix products, arithmetic and copies ran while one was open for 27% of the time, Pallas kernels for 0%

commit v1 on v0

--- a/solution.py
+++ b/solution.py
@@ -1,3 +1,4 @@
+import functools
 import math
 import jax
 import jax.numpy as jnp
@@ -12,6 +13,15 @@
 EPSILON = 1e-06
 MASKED = -1e30
 HIGHEST = lax.Precision.HIGHEST
+
+
+def heads_update(field_in, shard_axis, axis_name):
+    for hop_no in (shard_axis, axis_name):
+        field_in = lax.psum(field_in, axis_name=hop_no)
+    return field_in
+
+
+_arrange_quotas = functools.partial(heads_update, shard_axis=("ctx", "tp"), axis_name="shard")
 
 
 def unit_rows(values):
@@ -313,9 +323,8 @@
             0,
         )
 
-    alpha_attn_sum, alpha_mlp_sum, qk_sum, up_sum, gate_sum = lax.psum(
-        (sum_attn, sum_mlp, padded(sum_qk), padded(sum_up), padded(sum_gate)),
-        ("shard", "ctx", "tp"),
+    alpha_attn_sum, alpha_mlp_sum, qk_sum, up_sum, gate_sum = _arrange_quotas(
+        (sum_attn, sum_mlp, padded(sum_qk), padded(sum_up), padded(sum_gate))
     )
     return (
         jnp.stack([mid[m][0] for m in micros])[:, None],

time: 1380 us -> 1380 us (level)
  blocking collectives: 92.6 us -> 122 us
  waiting for transfers between devices: 707 us -> 678 us
    psum x1 -> x2, blocking collectives: 40.9 us -> 70.1 us  [heads_update(): field_in = lax.psum(field_in, axis_name=hop_no)]
    reduce_scatter x7, waiting for transfers between devices: 210 us -> 180 us  [to_owner(): lax.psum_scatter(product, spread, scatter_dimension=axis, tiled=True)]
where the time goes in v1:
time: 1380 us; the launch traced here: 1370 us
  waiting for transfers between devices  678 us (49%)
  matrix products  354 us (26%)
  blocking collectives  122 us (9%)
  local copies, waits for them, and re-layouts  111 us (8%)
  other arithmetic  84.3 us (6%)
  between operations  17.7 us (1%)
    reduce_scatter x8, waiting for transfers between devices, own_grads(): lax.psum_scatter(partial_value.astype(jnp.bfloat16), 'tp', scatter_dimens...  234 us
    reduce_scatter x7, waiting for transfers between devices, to_owner(): lax.psum_scatter(product, spread, scatter_dimension=axis, tiled=True)  180 us
    dot_general x44, matrix products, contract_cols(): lax.dot_general(former, latter, (((1,), (1,)), ((), ())), preferred_eleme...  127 us
    all_gather x4, waiting for transfers between devices, group_rows(): return lax.all_gather(own_block, 'tp', axis=0, tiled=True)  110 us
    dot_general x27, matrix products, contract_rows(): lax.dot_general(former, latter, (((0,), (0,)), ((), ())), preferred_eleme...  88.9 us
    all_gather x4, waiting for transfers between devices, group_grads(): return lax.all_gather(own_block, 'tp', axis=0, tiled=True)  71.4 us
    psum x2, blocking collectives, heads_update(): field_in = lax.psum(field_in, axis_name=hop_no)  70.1 us
    dot_general x10, matrix products, head_forward(): jnp.dot(soft_weights.astype(jnp.bfloat16), value_one, preferred_element_t...  49.6 us
  transfers between devices with their start and end apart: 30, of which 23 were waited for; matrix products, arithmetic and copies ran while one was open for 27% of the time, Pallas kernels for 0%

profile of v1, /device:TPU:0, one launch (start us, length us, event | category | flops | bytes accessed | tf_op | source)
XLA Modules:
  0.0 1370.8 jit_solution(6894940005163655728)
XLA Ops:
  54.6 36.5 %all-gather.38.cloned.1.call-done = bf16[1,1,640,1280]{3,2,1,0:T(8,128)(2,1)} async-done(((bf16[1,1,160,1280]{3,2,1,0:T(8,128)(2,1)}), bf16[1,1,640,1280]{3,2,1,0:T(8,128)(2,1)}) %all-gather.38.cloned.1.call-update) | async-done | bytes 1638416 | tf_op jit(solution)/shard_map/all_gather | solution.py:69
  150.4 57.9 %while.52 = (s32[]{:T(128)}, bf16[5,640,64]{1,2,0:T(8,128)(2,1)}, f32[5,640]{1,0:T(8,128)}, bf16[5,640,64]{2,1,0:T(8,128)(2,1)}, bf16[5,2560,64]{2,1,0:T(8,128)(...) while((s32[]{:T(128)}, bf16[5,640,64]{1,2,0:T(8,128)(2,1)}, ...), condition=%wide.region_5.6_spmd, body=%wide.region_2.5_spmd.sunk | while | flops 432536960 | bytes 49184892 | solution.py:142
  213.1 33.7 %reduce-scatter.22.cloned.1.call-done = bf16[160,1280]{1,0:T(8,128)(2,1)} async-done(((bf16[640,1280]{1,0:T(8,128)(2,1)}), bf16[160,1280]{1,0:T(8,128)(2,1)}) %reduce-scatter.22.cloned.1.call-update) | async-done | bytes 409616 | tf_op jit(solution)/shard_map/reduce_scatter | solution.py:81
  257.5 32.4 %all-gather.18.cloned.1.call-done = bf16[640,1280]{1,0:T(8,128)(2,1)} async-done(((bf16[160,1280]{1,0:T(8,128)(2,1)}), bf16[640,1280]{1,0:T(8,128)(2,1)}) %all-gather.18.cloned.1.call-update) | async-done | bytes 1638416 | tf_op jit(solution)/shard_map/all_gather | solution.py:69
  296.3 27.0 %all-gather.20.cloned.1.call-done = bf16[1280,1280]{1,0:T(8,128)(2,1)} async-done(((bf16[160,1280]{1,0:T(8,128)(2,1)}), bf16[1280,1280]{1,0:T(8,128)(2,1)}) %all-gather.20.cloned.1.call-update) | async-done | bytes 3276816 | tf_op jit(solution)/shard_map/all_gather | solution.py:272
  330.9 27.2 %all-gather.24.cloned.1.call-done = bf16[1280,1280]{0,1:T(8,128)(2,1)} async-done(((bf16[1280,160]{0,1:T(8,128)(2,1)}), bf16[1280,1280]{0,1:T(8,128)(2,1)}) %all-gather.24.cloned.1.call-update) | async-done | bytes 3276816 | tf_op jit(solution)/shard_map/all_gather | solution.py:274
  371.2 17.7 %all-gather.26.cloned.1.call-done = bf16[2560,640]{0,1:T(8,128)(2,1)} async-done(((bf16[640,640]{0,1:T(8,128)(2,1)}), bf16[2560,640]{0,1:T(8,128)(2,1)}) %all-gather.26.cloned.1.call-update) | async-done | bytes 3276816 | tf_op jit(solution)/shard_map/all_gather | solution.py:122
  409.1 51.7 %while.53 = (s32[]{:T(128)}, bf16[5,640,64]{1,2,0:T(8,128)(2,1)}, f32[5,640]{1,0:T(8,128)S(1)}, bf16[5,640,64]{2,1,0:T(8,128)(2,1)}, bf16[5,2560,64]{2,1,0:T(8,1...) while((s32[]{:T(128)}, bf16[5,640,64]{1,2,0:T(8,128)(2,1)}, ...), condition=%wide.region_17.18_spmd, body=%wide.region_14.17_spmd.sunk | while | flops 432536960 | bytes 49184892 | solution.py:142
  483.8 17.6 %reduce-scatter.26.cloned.1.call-done = bf16[160,1280]{1,0:T(8,128)(2,1)} async-done(((bf16[640,1280]{1,0:T(8,128)(2,1)}), bf16[160,1280]{1,0:T(8,128)(2,1)}) %reduce-scatter.26.cloned.1.call-update) | async-done | bytes 409616 | tf_op jit(solution)/shard_map/reduce_scatter | solution.py:81
  502.6 36.5 %reduce-scatter.30.cloned.1.call-done = bf16[160,1280]{1,0:T(8,128)(2,1)} async-done(((bf16[640,1280]{1,0:T(8,128)(2,1)}), bf16[160,1280]{1,0:T(8,128)(2,1)}) %reduce-scatter.30.cloned.1.call-update) | async-done | bytes 409616 | tf_op jit(solution)/shard_map/reduce_scatter | solution.py:81
  543.0 37.1 %all-gather.28.cloned.1.call-done = bf16[640,1280]{1,0:T(8,128)(2,1)} async-done(((bf16[160,1280]{1,0:T(8,128)(2,1)}), bf16[640,1280]{1,0:T(8,128)(2,1)}) %all-gather.28.cloned.1.call-update) | async-done | bytes 1638416 | tf_op jit(solution)/shard_map/all_gather | solution.py:69
  594.0 35.3 %reduce-scatter.28.cloned.1.call-done = bf16[160,1280]{1,0:T(8,128)(2,1)} async-done(((bf16[640,1280]{1,0:T(8,128)(2,1)}), bf16[160,1280]{1,0:T(8,128)(2,1)}) %reduce-scatter.28.cloned.1.call-update) | async-done | bytes 409616 | tf_op jit(solution)/shard_map/reduce_scatter | solution.py:81
  636.0 36.7 %all-gather.34.cloned.1.call-done = bf16[640,1280]{1,0:T(8,128)(2,1)} async-done(((bf16[160,1280]{1,0:T(8,128)(2,1)}), bf16[640,1280]{1,0:T(8,128)(2,1)}) %all-gather.34.cloned.1.call-update) | async-done | bytes 1638416 | tf_op jit(solution)/shard_map/all_gather | solution.py:73
  690.5 35.2 %reduce-scatter.34.cloned.1.call-done = bf16[160,1280]{1,0:T(8,128)(2,1)} async-done(((bf16[640,1280]{1,0:T(8,128)(2,1)}), bf16[160,1280]{1,0:T(8,128)(2,1)}) %reduce-scatter.34.cloned.1.call-update) | async-done | bytes 409616 | tf_op jit(solution)/shard_map/reduce_scatter | solution.py:81
  733.9 34.7 %all-gather.32.cloned.1.call-done = bf16[640,1280]{1,0:T(8,128)(2,1)} async-done(((bf16[160,1280]{1,0:T(8,128)(2,1)}), bf16[640,1280]{1,0:T(8,128)(2,1)}) %all-gather.32.cloned.1.call-update) | async-done | bytes 1638416 | tf_op jit(solution)/shard_map/all_gather | solution.py:73
  775.2 71.4 %while.54 = (s32[]{:T(128)}, f32[5,640,64]{1,2,0:T(8,128)S(1)}, bf16[5,2560,64]{1,2,0:T(8,128)(2,1)}, bf16[5,2560,64]{1,2,0:T(8,128)(2,1)}, bf16[5,640,64]{2,1,0...) while((s32[]{:T(128)}, f32[5,640,64]{1,2,0:T(8,128)S(1)}, ...), condition=%wide.region_31.32_spmd, body=%wide.region_29.31_spmd.sunk | while | flops 1063525760 | bytes 61458068 | solution.py:218
  860.5 71.4 %while.55 = (s32[]{:T(128)}, f32[5,640,64]{1,2,0:T(8,128)S(1)}, bf16[5,2560,64]{1,2,0:T(8,128)(2,1)}, bf16[5,2560,64]{1,2,0:T(8,128)(2,1)}, bf16[5,640,64]{2,1,0...) while((s32[]{:T(128)}, f32[5,640,64]{1,2,0:T(8,128)S(1)}, ...), condition=%wide.region_43.44_spmd, body=%wide.region_41.43_spmd.sunk | while | flops 1063525760 | bytes 61458068 | solution.py:218
  1028.5 48.2 %reduce-scatter.48.cloned.1.call-done = bf16[160,1280]{1,0:T(8,128)(2,1)} async-done(((bf16[1280,1280]{1,0:T(8,128)(2,1)}), bf16[160,1280]{1,0:T(8,128)(2,1)}) %reduce-scatter.48.cloned.1.call-update) | async-done | bytes 409616 | tf_op jit(solution)/shard_map/reduce_scatter | solution.py:300
  1078.7 48.2 %reduce-scatter.46.cloned.1.call-done = bf16[160,1280]{1,0:T(8,128)(2,1)} async-done(((bf16[1280,1280]{1,0:T(8,128)(2,1)}), bf16[160,1280]{1,0:T(8,128)(2,1)}) %reduce-scatter.46.cloned.1.call-update) | async-done | bytes 409616 | tf_op jit(solution)/shard_map/reduce_scatter | solution.py:300
  1129.0 36.7 %reduce-scatter.44.cloned.1.call-done = bf16[320,160]{0,1:T(8,128)(2,1)} async-done(((bf16[320,1280]{0,1:T(8,128)(2,1)}), bf16[320,160]{0,1:T(8,128)(2,1)}) %reduce-scatter.44.cloned.1.call-update) | async-done | bytes 102416 | tf_op jit(solution)/shard_map/reduce_scatter | solution.py:300
  1167.3 37.6 %reduce-scatter.38.cloned.1.call-done = bf16[160,320]{1,0:T(8,128)(2,1)} async-done(((bf16[1280,320]{1,0:T(8,128)(2,1)}), bf16[160,320]{1,0:T(8,128)(2,1)}) %reduce-scatter.38.cloned.1.call-update) | async-done | bytes 102416 | tf_op jit(solution)/shard_map/reduce_scatter | solution.py:300
  1206.6 61.5 %all-reduce = (f32[1280]{0:T(1024)S(1)}, f32[1280]{0:T(1024)S(1)}, f32[1280]{0:T(1024)S(1)}, f32[5120]{0:T(1024)S(1)}, f32[5120]{0:T(1024)S(1)}) all-reduce(f32[1280]{0:T(1024)S(1)} %add.338, f32[1280]{0:T(1024)S(1)} %add.339, f32[1280]{0:T(1024)S(1)} %add_dynamic-update-slice_fusion.1, ...), channel_id=1, replica_groups=mesh['shard'=2,'ctx'=4,'tp'=4] {'ctx','tp'}, use_global_device_ids=true, to_apply=%region_57.58 | all-reduce | flops 14080 | bytes 112640 | tf_op jit(solution)/shard_map/psum | solution.py:20
  1285.0 36.9 %reduce-scatter.36.cloned.1.call-done = bf16[160,1280]{1,0:T(8,128)(2,1)} async-done(((bf16[640,1280]{1,0:T(8,128)(2,1)}), bf16[160,1280]{1,0:T(8,128)(2,1)}) %reduce-scatter.36.cloned.1.call-update) | async-done | bytes 409616 | tf_op jit(solution)/shard_map/reduce_scatter | solution.py:81
  1321.9 38.3 %reduce-scatter.32.cloned.1.call-done = bf16[160,1280]{1,0:T(8,128)(2,1)} async-done(((bf16[640,1280]{1,0:T(8,128)(2,1)}), bf16[160,1280]{1,0:T(8,128)(2,1)}) %reduce-scatter.32.cloned.1.call-update) | async-done | bytes 409616 | tf_op jit(solution)/shard_map/reduce_scatter | solution.py:81
  (657 shorter events, 637.6 us)
Async XLA Ops:
  10.2 80.9 %all-gather.38.cloned.1.call-start = ((), (), s32[]{:S(2)}) async-start(), calls=%async_computation.43 | async-start | bytes 2048000 | tf_op jit(solution)/shard_map/all_gather | solution.py:69
  11.0 128.2 %all-gather.16.cloned.1.call-start = ((), (), s32[]{:S(2)}) async-start(), calls=%async_computation.17 | async-start | bytes 4096000 | tf_op jit(solution)/shard_map/all_gather | solution.py:122
  108.4 138.3 %reduce-scatter.22.cloned.1.call-start = ((), (), s32[]{:S(2)}) async-start(), calls=%async_computation.18 | async-start | bytes 2048000 | tf_op jit(solution)/shard_map/reduce_scatter | solution.py:81
  253.3 104.8 %all-gather.24.cloned.1.call-start = ((), (), s32[]{:S(2)}) async-start(), calls=%async_computation.22 | async-start | bytes 3686400 | tf_op jit(solution)/shard_map/all_gather | solution.py:274
  254.0 134.9 %all-gather.26.cloned.1.call-start = ((), (), s32[]{:S(2)}) async-start(), calls=%async_computation.24 | async-start | bytes 4096000 | tf_op jit(solution)/shard_map/all_gather | solution.py:122
  257.3 144.4 %reduce-scatter.24.cloned.1.call-start = ((), (), s32[]{:S(2)}) async-start(), calls=%async_computation.23 | async-start | bytes 2048000 | tf_op jit(solution)/shard_map/reduce_scatter | solution.py:81
  364.0 101.3 %all-gather.30.cloned.1.call-start = ((), (), s32[]{:S(2)}) async-start(), calls=%async_computation.28 | async-start | bytes 2048000 | tf_op jit(solution)/shard_map/all_gather | solution.py:73
  409.0 92.4 %reduce-scatter.26.cloned.1.call-start = ((), (), s32[]{:S(2)}) async-start(), calls=%async_computation.25 | async-start | bytes 2048000 | tf_op jit(solution)/shard_map/reduce_scatter | solution.py:81
  483.7 96.4 %all-gather.28.cloned.1.call-start = ((), (), s32[]{:S(2)}) async-start(), calls=%async_computation.26 | async-start | bytes 2048000 | tf_op jit(solution)/shard_map/all_gather | solution.py:69
  543.0 86.3 %reduce-scatter.28.cloned.1.call-start = ((), (), s32[]{:S(2)}) async-start(), calls=%async_computation.27 | async-start | bytes 2048000 | tf_op jit(solution)/shard_map/reduce_scatter | solution.py:81
  593.9 78.7 %all-gather.34.cloned.1.call-start = ((), (), s32[]{:S(2)}) async-start(), calls=%async_computation.32 | async-start | bytes 2048000 | tf_op jit(solution)/shard_map/all_gather | solution.py:73
  635.5 90.2 %reduce-scatter.34.cloned.1.call-start = ((), (), s32[]{:S(2)}) async-start(), calls=%async_computation.33 | async-start | bytes 2048000 | tf_op jit(solution)/shard_map/reduce_scatter | solution.py:81
  731.5 121.9 %all-gather.36.cloned.1.call-start = ((), (), s32[]{:S(2)}) async-start(), calls=%async_computation.34 | async-start | bytes 2048000 | tf_op jit(solution)/shard_map/all_gather | solution.py:73
  733.7 245.9 %reduce-scatter.52.cloned.1.call-start = ((), (), s32[]{:S(2)}) async-start(), calls=%async_computation.45 | async-start | bytes 4096000
  853.1 128.8 %reduce-scatter.54.cloned.1.call-start = ((), (), s32[]{:S(2)}) async-start(), calls=%async_computation.46 | async-start | bytes 4096000
  938.4 88.1 %reduce-scatter.50.cloned.1.call-start = ((), (), s32[]{:S(2)}) async-start(), calls=%async_computation.42 | async-start | bytes 3686400 | tf_op jit(solution)/shard_map/reduce_scatter | solution.py:300
  948.2 128.5 %reduce-scatter.48.cloned.1.call-start = ((), (), s32[]{:S(2)}) async-start(), calls=%async_computation.41 | async-start | bytes 3686400 | tf_op jit(solution)/shard_map/reduce_scatter | solution.py:300
  958.9 168.0 %reduce-scatter.46.cloned.1.call-start = ((), (), s32[]{:S(2)}) async-start(), calls=%async_computation.40 | async-start | bytes 3686400 | tf_op jit(solution)/shard_map/reduce_scatter | solution.py:300
  968.8 197.0 %reduce-scatter.44.cloned.1.call-start = ((), (), s32[]{:S(2)}) async-start(), calls=%async_computation.39 | async-start | bytes 1105920 | tf_op jit(solution)/shard_map/reduce_scatter | solution.py:300
  974.1 230.8 %reduce-scatter.38.cloned.1.call-start = ((), (), s32[]{:S(2)}) async-start(), calls=%async_computation.36 | async-start | bytes 1105920 | tf_op jit(solution)/shard_map/reduce_scatter | solution.py:300
  979.0 299.7 %reduce-scatter.42.cloned.1.call-start = ((), (), s32[]{:S(2)}) async-start(), calls=%async_computation.38 | async-start | bytes 1105920 | tf_op jit(solution)/shard_map/reduce_scatter | solution.py:300
  990.2 293.2 %reduce-scatter.40.cloned.1.call-start = ((), (), s32[]{:S(2)}) async-start(), calls=%async_computation.37 | async-start | bytes 1105920 | tf_op jit(solution)/shard_map/reduce_scatter | solution.py:300
  1007.3 314.6 %reduce-scatter.36.cloned.1.call-start = ((), (), s32[]{:S(2)}) async-start(), calls=%async_computation.35 | async-start | bytes 2048000 | tf_op jit(solution)/shard_map/reduce_scatter | solution.py:81
  1012.4 347.9 %reduce-scatter.32.cloned.1.call-start = ((), (), s32[]{:S(2)}) async-start(), calls=%async_computation.31 | async-start | bytes 2048000 | tf_op jit(solution)/shard_map/reduce_scatter | solution.py:81
  (145 other events, 2729.7 us)
Sparse Core Ops, SparseCore 0:
  11.0 40.8 all-gather.39
  54.0 37.0 all-gather.37
  108.5 30.6 all-gather.15
  212.0 34.6 reduce-scatter.21
  364.1 36.3 reduce-scatter.23
  409.1 38.1 all-gather.29
  465.1 36.2 reduce-scatter.25
  503.8 35.3 reduce-scatter.29
  594.1 35.1 reduce-scatter.27
  690.6 35.1 reduce-scatter.33
  853.2 37.6 reduce-scatter.51
  938.5 37.6 reduce-scatter.53
  979.6 46.8 reduce-scatter.49
  1029.8 46.8 reduce-scatter.47
  1080.0 46.8 reduce-scatter.45
  1129.9 35.7 reduce-scatter.43
  1169.1 35.7 reduce-scatter.37
  1208.0 35.7 reduce-scatter.41
  1247.3 36.0 reduce-scatter.39
  1285.6 36.2 reduce-scatter.35
  1324.9 35.3 reduce-scatter.31
Sparse Core Ops, SparseCore 1:
  214.4 31.0 all-gather.21
  252.7 37.0 all-gather.17
  291.7 31.5 all-gather.19
  325.4 32.7 all-gather.23
  359.7 29.1 all-gather.25
  543.1 37.0 all-gather.27
  635.6 37.0 all-gather.33
  731.5 37.0 all-gather.31
  770.1 36.8 all-gather.35
